TPU v7x, 32 devices: a whole 2x2x4 slice. The times are simulated.
32 devices in a mesh: sec: 4 (over x, core), dp: 2 (over y), mp: 4 (over z).
Axes of the slice: x: 2, y: 2, z: 4, core: 2. Of those that a mesh axis runs over, the one named last changes fastest.
Arguments:
- queries: bfloat16 [1024, 8192], P(('sec', 'dp'), 'mp'), may hold values from -6 to 6
- cotangent: bfloat16 [1024, 8192], P(('sec', 'dp'), 'mp'), may hold values from -6 to 6
- keys_raw: bfloat16 [80, 48, 1024], P(('sec', 'dp'), None, 'mp'), may hold values from -6 to 6
- values: bfloat16 [80, 48, 1024], P(('sec', 'dp'), None, 'mp'), may hold values from -6 to 6
- image_counts: int32 [32], P(('sec', 'dp')), may hold values from 1 to 4, as said below
- image_route: int32 [80], P(('sec', 'dp')), may hold values from 0 to 127, as said below
- text_lengths: int32 [32], P(('sec', 'dp')), may hold values from 1 to 32, as said below
- q_gain: float32 [128], replicated
- k_gain: float32 [128], replicated
Outputs:
- query_grad: bfloat16 [1024, 8192], P(('sec', 'dp'), 'mp')
- key_grad: bfloat16 [80, 48, 1024], P(('sec', 'dp'), None, 'mp')
- value_grad: bfloat16 [80, 48, 1024], P(('sec', 'dp'), None, 'mp')
- q_gain_grad: float32 [128], replicated
- k_gain_grad: float32 [128], replicated
Inputs may be any that keep to these rules, and one draw needn't show every extreme that they name: `image_counts`: the counts of the 8 sequences of one index of sec sum to 20. `image_route`: each pair (s, k) with k < image_counts[s] appears exactly once; the images of an index of sec belong to sequences of that index; of the images of one device, at most 8 belong to the sequences of any one device, and this is reached. `text_lengths`: some sequence of every device has 32 live tokens.
All inputs are finite; a program needn't handle non-finite values.
Results may differ from a plain program's by a relative error of at most 0.01.
The roundings to bfloat16 on the way count: a program that leaves them out, or rounds other values in their place, can miss the bound.
Values may be sent and summed in bfloat16 or wider, within the bound.
A program may use at most 64 MiB of HBM per device.

v0:
```python
import jax
import jax.numpy as jnp
from jax import lax
from jax.sharding import PartitionSpec as P


def norm_forward(inputs, norm_gain):
    wide = inputs.astype(jnp.float32)
    inv_rms = lax.rsqrt(jnp.mean(wide * wide, axis=-1, keepdims=True) + 1e-05)
    return (wide * inv_rms * norm_gain).astype(jnp.bfloat16)


def norm_backward(inputs, norm_gain, upstream):
    wide = inputs.astype(jnp.float32)
    inv_rms = lax.rsqrt(jnp.mean(wide * wide, axis=-1, keepdims=True) + 1e-05)
    scaled = norm_gain * upstream
    grad_in = inv_rms * scaled - wide * inv_rms**3 * jnp.mean(wide * scaled, axis=-1, keepdims=True)
    gain_grad = jnp.sum((upstream * wide * inv_rms).reshape(-1, inputs.shape[-1]), axis=0)
    return (grad_in.astype(jnp.bfloat16), gain_grad)


def attend(query_norm, slot_keys, slot_vals, live_keys, grad, scaling):
    scores = (
        jnp.einsum("slkgd,sjkd->skglj", query_norm, slot_keys, preferred_element_type=jnp.float32)
        * scaling
    )
    scores = jnp.where(live_keys[:, None, None, None, :], scores, -1e30)
    row_top = jnp.max(scores, axis=-1, keepdims=True)
    expo = jnp.exp(scores - row_top)
    probs = expo / jnp.sum(expo, axis=-1, keepdims=True)
    probs_low = probs.astype(jnp.bfloat16)
    output = jnp.einsum(
        "skglj,sjkd->slkgd", probs_low, slot_vals, preferred_element_type=jnp.float32
    )
    dprob = jnp.einsum("slkgd,sjkd->skglj", grad, slot_vals, preferred_element_type=jnp.float32)
    row_dots = jnp.transpose(jnp.sum(grad.astype(jnp.float32) * output, axis=-1), (0, 2, 3, 1))
    dscore = (probs * (dprob - row_dots[..., None])).astype(jnp.bfloat16)
    dq_norm = (
        jnp.einsum("skglj,sjkd->slkgd", dscore, slot_keys, preferred_element_type=jnp.float32)
        * scaling
    )
    dk_slots = (
        jnp.einsum("skglj,slkgd->sjkd", dscore, query_norm, preferred_element_type=jnp.float32)
        * scaling
    ).astype(jnp.bfloat16)
    dv_slots = jnp.einsum(
        "skglj,slkgd->sjkd", probs_low, grad, preferred_element_type=jnp.float32
    ).astype(jnp.bfloat16)
    return (dq_norm, dk_slots, dv_slots)


def on_device(
    queries, cotangent, keys_raw, values, image_counts, image_route, text_lengths, q_gain, k_gain
):
    dp_count = lax.axis_size("dp")
    seq_dev = image_counts.shape[0]
    img_dev = keys_raw.shape[0]
    patches = keys_raw.shape[1]
    kv_width = keys_raw.shape[2]
    head_dim = q_gain.shape[0]
    kv_local = kv_width // head_dim
    tokens = queries.shape[0]
    seq_len = tokens // seq_dev
    q_per_kv = queries.shape[1] // head_dim // kv_local
    capacity = (4 * seq_dev + dp_count - 1) // dp_count
    cells = dp_count * capacity
    scaling = head_dim ** (-0.5)
    first_seq = (lax.axis_index("sec") * dp_count + lax.axis_index("dp")) * seq_dev
    target_dev = image_route // 4 // seq_dev % dp_count
    same_target = target_dev[:, None] == target_dev[None, :]
    earlier = jnp.arange(img_dev)[None, :] < jnp.arange(img_dev)[:, None]
    order_in = jnp.sum((same_target & earlier).astype(jnp.int32), axis=1)
    target = target_dev * capacity + order_in
    placing_bool = target[:, None] == jnp.arange(cells)[None, :]
    placing = placing_bool.astype(jnp.bfloat16)
    route_send = jnp.sum(jnp.where(placing_bool, image_route[:, None] + 1, 0), axis=0) - 1
    key_source = norm_forward(
        keys_raw.reshape(img_dev, patches, kv_local, head_dim), k_gain
    ).reshape(img_dev, patches, kv_width)
    send_keys = jnp.einsum(
        "ic,ipw->cpw", placing, key_source, preferred_element_type=jnp.float32
    ).astype(jnp.bfloat16)
    send_vals = jnp.einsum(
        "ic,ipw->cpw", placing, values, preferred_element_type=jnp.float32
    ).astype(jnp.bfloat16)
    recv_keys, recv_vals, recv_route = (
        lax.all_to_all(
            send_keys.reshape(dp_count, capacity, patches, kv_width),
            "dp",
            split_axis=0,
            concat_axis=0,
            tiled=True,
        ),
        lax.all_to_all(
            send_vals.reshape(dp_count, capacity, patches, kv_width),
            "dp",
            split_axis=0,
            concat_axis=0,
            tiled=True,
        ),
        lax.all_to_all(
            route_send.reshape(dp_count, capacity), "dp", split_axis=0, concat_axis=0, tiled=True
        ),
    )
    recv_keys = recv_keys.reshape(cells, patches, kv_width)
    recv_vals = recv_vals.reshape(cells, patches, kv_width)
    recv_route = recv_route.reshape(cells)
    select = (recv_route[None, :] - 4 * first_seq == jnp.arange(4 * seq_dev)[:, None]).astype(
        jnp.bfloat16
    )
    slot_keys = jnp.einsum(
        "qr,rpw->qpw", select, recv_keys, preferred_element_type=jnp.float32
    ).astype(jnp.bfloat16)
    slot_vals = jnp.einsum(
        "qr,rpw->qpw", select, recv_vals, preferred_element_type=jnp.float32
    ).astype(jnp.bfloat16)
    slot_keys = slot_keys.reshape(seq_dev, 4 * patches, kv_local, head_dim)
    slot_vals = slot_vals.reshape(seq_dev, 4 * patches, kv_local, head_dim)
    q_heads = queries.reshape(seq_dev, seq_len, kv_local, q_per_kv, head_dim)
    query_norm = norm_forward(q_heads, q_gain)
    live_rows = jnp.arange(seq_len)[None, :] < text_lengths[:, None]
    grad = jnp.where(
        live_rows[:, :, None, None, None],
        cotangent.reshape(seq_dev, seq_len, kv_local, q_per_kv, head_dim),
        0,
    )
    live_keys = (jnp.arange(4 * patches) // patches)[None, :] < image_counts[:, None]
    dq_norm, dk_slots, dv_slots = attend(query_norm, slot_keys, slot_vals, live_keys, grad, scaling)
    back_keys = jnp.einsum(
        "qr,qpw->rpw",
        select,
        dk_slots.reshape(4 * seq_dev, patches, kv_width),
        preferred_element_type=jnp.float32,
    ).astype(jnp.bfloat16)
    back_vals = jnp.einsum(
        "qr,qpw->rpw",
        select,
        dv_slots.reshape(4 * seq_dev, patches, kv_width),
        preferred_element_type=jnp.float32,
    ).astype(jnp.bfloat16)
    home_keys, home_vals = (
        lax.all_to_all(
            back_keys.reshape(dp_count, capacity, patches, kv_width),
            "dp",
            split_axis=0,
            concat_axis=0,
            tiled=True,
        ),
        lax.all_to_all(
            back_vals.reshape(dp_count, capacity, patches, kv_width),
            "dp",
            split_axis=0,
            concat_axis=0,
            tiled=True,
        ),
    )
    home_keys = jnp.einsum(
        "ic,cpw->ipw",
        placing,
        home_keys.reshape(cells, patches, kv_width),
        preferred_element_type=jnp.float32,
    ).astype(jnp.bfloat16)
    value_grad = jnp.einsum(
        "ic,cpw->ipw",
        placing,
        home_vals.reshape(cells, patches, kv_width),
        preferred_element_type=jnp.float32,
    ).astype(jnp.bfloat16)
    key_grad, k_part = norm_backward(
        keys_raw.reshape(img_dev, patches, kv_local, head_dim),
        k_gain,
        home_keys.reshape(img_dev, patches, kv_local, head_dim).astype(jnp.float32),
    )
    key_grad = key_grad.reshape(img_dev, patches, kv_width)
    query_grad, q_part = norm_backward(q_heads, q_gain, dq_norm)
    q_gain_grad, k_gain_grad = lax.psum((q_part, k_part), ("sec", "dp", "mp"))
    return (
        query_grad.reshape(tokens, queries.shape[1]),
        key_grad,
        value_grad,
        q_gain_grad,
        k_gain_grad,
    )


def solution(mesh):
    placed = (
        P(("sec", "dp"), "mp"),
        P(("sec", "dp"), "mp"),
        P(("sec", "dp"), None, "mp"),
        P(("sec", "dp"), None, "mp"),
        P(("sec", "dp")),
        P(("sec", "dp")),
        P(("sec", "dp")),
        P(),
        P(),
    )
    return jax.shard_map(
        on_device,
        mesh=mesh,
        in_specs=placed,
        out_specs=(
            P(("sec", "dp"), "mp"),
            P(("sec", "dp"), None, "mp"),
            P(("sec", "dp"), None, "mp"),
            P(),
            P(),
        ),
        check_vma=False,
    )
```

profile of v0, /device:TPU:0, one launch (start us, length us, event | category | flops | bytes accessed | tf_op | source)
XLA Modules:
  0.0 110.6 jit_solution(13246118657336125844)
XLA Ops:
  0.6 0.7 broadcast_add_fusion.1
  1.7 0.6 sub.58
  2.3 4.3 %all-to-all-start = ((s32[2,1,8]{2,1,0:T(1,128)}), s32[2,1,8]{2,1,0:T(1,128)S(1)}, u32[]{:S(2)}, u32[]{:S(2)}) async-start(s32[2,1,8]{2,1,0:T(1,128)} %bitcast), calls=%async_computation | async-start | bytes 2048 | tf_op jit(solution)/shard_map/all_to_all | solution.py:101
  6.6 1.1 %convert_bitcast_fusion = f32[16,8,16,128]{3,1,2,0:T(8,128)S(1)} fusion(bf16[128,2048]{1,0:T(8,128)(2,1)} %param.9), kind=kLoop, calls=%fused_computation.38 | loop fusion | flops 262144 | bytes 1572864
  8.0 0.4 multiply_reduce_fusion
  8.6 0.4 fusion.14
  9.0 0.8 copy.194
  9.7 0.9 copy.239
  11.0 0.6 multiply_reduce_fusion.3
  11.8 0.6 mul.201
  12.4 0.4 mul.202
  12.9 3.5 %all-to-all-start.2 = ((bf16[2,8,48,256]{3,1,2,0:T(8,128)(2,1)}), bf16[2,8,48,256]{3,1,2,0:T(8,128)(2,1)S(1)}, u32[]{:S(2)}, u32[]{:S(2)}) async-start(bf16[2,8,48,256]{3,1,2,0:T(8,128)(2,1)} %copy.194), calls=%async_computation.2 | async-start | bytes 786432 | tf_op jit(solution)/shard_map/all_to_all | solution.py:94
  16.4 0.4 fusion.13
  16.8 0.8 copy.186
  17.6 0.6 mul.230
  18.2 1.2 %mul.231 = f32[10,48,256]{2,1,0:T(8,128)} reshape(f32[10,48,2,128]{3,2,1,0:T(2,128)S(1)} %mul.230) | data formatting | bytes 983040 | tf_op jit(solution)/shard_map/mul | solution.py:17
  19.4 4.0 %all-to-all-done.2 = bf16[2,8,48,256]{3,1,2,0:T(8,128)(2,1)S(1)} async-done(((bf16[2,8,48,256]{3,1,2,0:T(8,128)(2,1)}), bf16[2,8,48,256]{3,1,2,0:T(8,128)(2,1)S(1)}, u32[]{:S(2)}, u32[]{:S(2)}) %all-to-all-start.2) | async-done | bytes 393248 | tf_op jit(solution)/shard_map/all_to_all | solution.py:94
  23.5 3.5 %all-to-all-start.1 = ((bf16[2,8,48,256]{3,1,2,0:T(8,128)(2,1)}), bf16[2,8,48,256]{3,1,2,0:T(8,128)(2,1)S(1)}, u32[]{:S(2)}, u32[]{:S(2)}) async-start(bf16[2,8,48,256]{3,1,2,0:T(8,128)(2,1)} %copy.186), calls=%async_computation.1 | async-start | bytes 786432 | tf_op jit(solution)/shard_map/all_to_all | solution.py:87
  27.4 0.8 reshape.219
  28.3 4.8 %all-to-all-done.1 = bf16[2,8,48,256]{3,1,2,0:T(8,128)(2,1)S(1)} async-done(((bf16[2,8,48,256]{3,1,2,0:T(8,128)(2,1)}), bf16[2,8,48,256]{3,1,2,0:T(8,128)(2,1)S(1)}, u32[]{:S(2)}, u32[]{:S(2)}) %all-to-all-start.1) | async-done | bytes 393248 | tf_op jit(solution)/shard_map/all_to_all | solution.py:87
  33.7 0.6 fusion.42
  34.3 1.1 fusion.76
  35.4 1.8 %fusion.12 = bf16[4,192,2,128]{3,1,2,0:T(8,128)(2,1)} fusion(bf16[4,32,2,8,128]{4,3,2,1,0:T(8,128)(2,1)S(1)} %bitcast.121, pred[4,32]{1,0:T(4,128)(4,1)S(1)} %iota_compare_fusion.3, f32[4,2,8,32,192]{4,3,2,1,0:T(8,128)S(1)} %get-tuple-element.48, f32[4,2,8,32]{3,2,1,0:T(8,128)S(1)} %get-tuple-element.47), kind=kOutput, calls=%fused_computation.24 | convolution fusion | flops 101908480 | bytes 2498688 | tf_op jit(solution)/shard_map/skglj,slkgd->sjkd/dot_general | solution.py:46
  37.3 0.7 fusion.11
  38.0 0.8 fusion.2
  38.8 0.9 fusion.17
  39.8 0.9 fusion.19
  40.7 1.2 %copy.205 = bf16[4,192,2,128]{3,2,1,0:T(2,128)(2,1)} copy(bf16[4,192,2,128]{3,1,2,0:T(8,128)(2,1)S(1)} %fusion.17) | data formatting | bytes 786432 | tf_op jit(solution)/shard_map/convert_element_type | solution.py:45
  41.9 2.0 %reshape.222 = bf16[16,48,256]{2,1,0:T(8,128)(2,1)} reshape(bf16[4,192,2,128]{3,2,1,0:T(2,128)(2,1)} %copy.205) | data formatting | bytes 786432 | tf_op jit(solution)/shard_map/reshape | solution.py:132
  43.9 1.3 %fusion.15 = bf16[2,8,48,256]{3,1,0,2:T(8,128)(2,1)S(1)} fusion(bf16[16,48,256]{2,1,0:T(8,128)(2,1)} %reshape.222, s32[16]{0:T(128)S(1)} %sub.61), kind=kOutput, calls=%fused_computation.27 | convolution fusion | flops 6488320 | bytes 786496 | tf_op jit(solution)/shard_map/qr,qpw->rpw/dot_general | solution.py:129
  45.2 0.8 copy.207
  46.0 4.3 %all-to-all-start.3 = ((bf16[2,8,48,256]{3,1,2,0:T(8,128)(2,1)}), bf16[2,8,48,256]{3,1,2,0:T(8,128)(2,1)}, u32[]{:S(2)}, u32[]{:S(2)}) async-start(bf16[2,8,48,256]{3,1,2,0:T(8,128)(2,1)} %copy.207), calls=%async_computation.3 | async-start | bytes 786432 | tf_op jit(solution)/shard_map/all_to_all | solution.py:142
  50.3 1.0 fusion.21
  51.5 1.0 reshape.221
  52.6 0.4 copy.210
  53.6 0.8 copy.212
  54.3 1.8 %all-to-all-done.3 = bf16[2,8,48,256]{3,1,2,0:T(8,128)(2,1)} async-done(((bf16[2,8,48,256]{3,1,2,0:T(8,128)(2,1)}), bf16[2,8,48,256]{3,1,2,0:T(8,128)(2,1)}, u32[]{:S(2)}, u32[]{:S(2)}) %all-to-all-start.3) | async-done | bytes 393248 | tf_op jit(solution)/shard_map/all_to_all | solution.py:142
  56.1 4.1 %all-to-all-start.4 = ((bf16[2,8,48,256]{3,1,2,0:T(8,128)(2,1)}), bf16[2,8,48,256]{3,1,2,0:T(8,128)(2,1)}, u32[]{:S(2)}, u32[]{:S(2)}) async-start(bf16[2,8,48,256]{3,1,2,0:T(8,128)(2,1)} %copy.212), calls=%async_computation.4 | async-start | bytes 786432 | tf_op jit(solution)/shard_map/all_to_all | solution.py:149
  60.3 1.3 %fusion.28 = bf16[10,48,256]{2,0,1:T(8,128)(2,1)S(1)} fusion(bf16[2,8,48,256]{3,1,2,0:T(8,128)(2,1)} %all-to-all-done.3, s32[10]{0:T(128)S(1)} %multiply_add_fusion), kind=kOutput, calls=%fused_computation.54 | convolution fusion | flops 3932320 | bytes 639016 | tf_op jit(solution)/shard_map/ic,cpw->ipw/dot_general | solution.py:157
  62.0 0.6 multiply_reduce_fusion.2
  62.6 1.4 %mul.236 = f32[10,48,2,128]{3,2,1,0:T(2,128)} broadcast(f32[10,48,2]{2,1,0:T(8,128)S(1)} %broadcast_multiply_fusion), dimensions={0,1,2} | broadcast | bytes 495360 | tf_op jit(solution)/shard_map/mul | solution.py:17
  64.0 1.4 %mul.237 = f32[10,48,256]{2,1,0:T(8,128)S(1)} reshape(f32[10,48,2,128]{3,2,1,0:T(2,128)} %mul.236) | data formatting | bytes 983040 | tf_op jit(solution)/shard_map/mul | solution.py:17
  65.4 0.8 all-to-all-done.4
  66.2 1.3 %convolution_convert_fusion = bf16[10,48,256]{2,0,1:T(8,128)(2,1)S(1)} fusion(bf16[2,8,48,256]{3,1,2,0:T(8,128)(2,1)} %all-to-all-done.4, s32[10]{0:T(128)S(1)} %multiply_add_fusion), kind=kOutput, calls=%fused_computation.15 | convolution fusion | flops 4055200 | bytes 639016 | tf_op jit(solution)/shard_map/ic,cpw->ipw/dot_general | solution.py:163
  67.5 0.8 copy.215
  68.3 0.8 mul.245
  69.1 0.9 subtract_convert_fusion
  70.4 40.2 %all-reduce = (f32[128]{0:T(128)}, f32[128]{0:T(128)}) all-reduce(f32[128]{0:T(128)S(1)} %get-tuple-element.35, f32[128]{0:T(128)S(1)} %multiply_reduce_fusion.1), channel_id=1, replica_groups=mesh['sec'=4,'dp'=2,'mp'=4] {'sec','dp','mp'}, use_global_device_ids=true, to_apply=%region_10.11 | all-reduce | flops 256 | bytes 2048 | tf_op jit(solution)/shard_map/psum | solution.py:176
  (62 shorter events, 4.1 us)
Async XLA Ops:
  0.6 7.9 %copy-start = (bf16[10,48,256]{2,1,0:T(8,128)(2,1)S(1)}, bf16[10,48,256]{2,1,0:T(8,128)(2,1)}, u32[]{:S(2)}) copy-start(bf16[10,48,256]{2,1,0:T(8,128)(2,1)} %param.12) | copy-start | bytes 737284
  2.3 10.6 %all-to-all-start = ((s32[2,1,8]{2,1,0:T(1,128)}), s32[2,1,8]{2,1,0:T(1,128)S(1)}, u32[]{:S(2)}, u32[]{:S(2)}) async-start(s32[2,1,8]{2,1,0:T(1,128)} %bitcast), calls=%async_computation | async-start | bytes 2048 | tf_op jit(solution)/shard_map/all_to_all | solution.py:101
  7.7 0.8 copy-start.11
  7.7 2.0 %copy-start.7 = (bf16[128,2048]{1,0:T(8,128)(2,1)S(1)}, bf16[128,2048]{1,0:T(8,128)(2,1)}, u32[]{:S(2)}) copy-start(bf16[128,2048]{1,0:T(8,128)(2,1)} %param.10) | copy-start | bytes 1572868
  7.9 2.7 %copy-start.14 = (s32[4]{0:T(128)S(1)}, s32[4]{0:T(128)}, u32[]{:S(2)}) copy-start(s32[4]{0:T(128)} %param.15) | copy-start | bytes 52
  8.0 2.8 %copy-start.1 = (bf16[10,48,256]{2,1,0:T(8,128)(2,1)S(1)}, bf16[10,48,256]{2,1,0:T(8,128)(2,1)}, u32[]{:S(2)}) copy-start(bf16[10,48,256]{2,1,0:T(8,128)(2,1)} %param.11) | copy-start | bytes 737284
  10.7 2.1 %copy-start.12 = (f32[128]{0:T(128)S(1)}, f32[128]{0:T(128)}, u32[]{:S(2)}) copy-start(f32[128]{0:T(128)} %param.17) | copy-start | bytes 1540
  11.0 1.9 %copy-start.13 = (s32[4]{0:T(128)S(1)}, s32[4]{0:T(128)}, u32[]{:S(2)}) copy-start(s32[4]{0:T(128)} %param.13) | copy-start | bytes 52
  12.9 10.5 %all-to-all-start.2 = ((bf16[2,8,48,256]{3,1,2,0:T(8,128)(2,1)}), bf16[2,8,48,256]{3,1,2,0:T(8,128)(2,1)S(1)}, u32[]{:S(2)}, u32[]{:S(2)}) async-start(bf16[2,8,48,256]{3,1,2,0:T(8,128)(2,1)} %copy.194), calls=%async_computation.2 | async-start | bytes 786432 | tf_op jit(solution)/shard_map/all_to_all | solution.py:94
  23.5 9.6 %all-to-all-start.1 = ((bf16[2,8,48,256]{3,1,2,0:T(8,128)(2,1)}), bf16[2,8,48,256]{3,1,2,0:T(8,128)(2,1)S(1)}, u32[]{:S(2)}, u32[]{:S(2)}) async-start(bf16[2,8,48,256]{3,1,2,0:T(8,128)(2,1)} %copy.186), calls=%async_computation.1 | async-start | bytes 786432 | tf_op jit(solution)/shard_map/all_to_all | solution.py:87
  33.7 1.7 %copy-start.3 = (bf16[4,192,2,128]{3,2,1,0:T(2,128)(2,1)}, bf16[4,192,2,128]{3,2,1,0:T(2,128)(2,1)S(1)}, u32[]{:S(2)}) copy-start(bf16[4,192,2,128]{3,2,1,0:T(2,128)(2,1)S(1)} %reshape.216) | copy-start | bytes 1179652
  34.3 1.1 %copy-start.8 = (bf16[16,8,16,128]{3,2,1,0:T(8,128)(2,1)S(1)}, bf16[16,8,16,128]{3,2,1,0:T(8,128)(2,1)}, u32[]{:S(2)}) copy-start(bf16[16,8,16,128]{3,2,1,0:T(8,128)(2,1)} %copy.239) | copy-start | bytes 1572868
  35.4 1.8 %copy-start.10 = (bf16[4,192,2,128]{3,2,1,0:T(2,128)(2,1)S(1)}, bf16[4,192,2,128]{3,2,1,0:T(2,128)(2,1)}, u32[]{:S(2)}) copy-start(bf16[4,192,2,128]{3,2,1,0:T(2,128)(2,1)} %reshape.219) | copy-start | bytes 1179652
  38.8 1.0 copy-start.4
  46.0 10.1 %all-to-all-start.3 = ((bf16[2,8,48,256]{3,1,2,0:T(8,128)(2,1)}), bf16[2,8,48,256]{3,1,2,0:T(8,128)(2,1)}, u32[]{:S(2)}, u32[]{:S(2)}) async-start(bf16[2,8,48,256]{3,1,2,0:T(8,128)(2,1)} %copy.207), calls=%async_computation.3 | async-start | bytes 786432 | tf_op jit(solution)/shard_map/all_to_all | solution.py:142
  51.3 1.2 %copy-start.9 = (bf16[4,192,2,128]{3,1,2,0:T(8,128)(2,1)S(1)}, bf16[4,192,2,128]{3,1,2,0:T(8,128)(2,1)}, u32[]{:S(2)}) copy-start(bf16[4,192,2,128]{3,1,2,0:T(8,128)(2,1)} %fusion.12) | copy-start | bytes 1179652
  53.0 8.6 %copy-start.2 = (bf16[10,48,256]{2,1,0:T(8,128)(2,1)S(1)}, bf16[10,48,256]{2,1,0:T(8,128)(2,1)}, u32[]{:S(2)}) copy-start(bf16[10,48,256]{2,1,0:T(8,128)(2,1)} %param.11) | copy-start | bytes 737284
  56.1 10.1 %all-to-all-start.4 = ((bf16[2,8,48,256]{3,1,2,0:T(8,128)(2,1)}), bf16[2,8,48,256]{3,1,2,0:T(8,128)(2,1)}, u32[]{:S(2)}, u32[]{:S(2)}) async-start(bf16[2,8,48,256]{3,1,2,0:T(8,128)(2,1)} %copy.212), calls=%async_computation.4 | async-start | bytes 786432 | tf_op jit(solution)/shard_map/all_to_all | solution.py:149
  62.6 6.5 %copy-start.5 = (f32[10,48,256]{2,1,0:T(8,128)S(1)}, f32[10,48,256]{2,1,0:T(8,128)}, u32[]{:S(2)}) copy-start(f32[10,48,256]{2,1,0:T(8,128)} %mul.231) | copy-start | bytes 1474564
  69.1 1.0 copy-start.6
where the time goes:
time: 111 us
  blocking collectives  40.2 us (36%)
  starting transfers between devices  19.7 us (18%)
  local copies, waits for them, and re-layouts  19.2 us (17%)
  matrix products  11.5 us (10%)
  waiting for transfers between devices  11.4 us (10%)
  other arithmetic  7.4 us (7%)
  between operations  1.17 us (1%)
    psum x1, blocking collectives, on_device(): q_gain_grad, k_gain_grad = lax.psum((q_part, k_part), ('sec', 'dp', 'mp'))  40.2 us
    all_to_all x1, waiting for transfers between devices, on_device(): lax.all_to_all(send_keys.reshape(dp_count, capacity, patches, kv_width),...  4.81 us
    mul x4, local copies, waits for them, and re-layouts, norm_backward(): wide * inv_rms ** 3 * jnp.mean(wide * scaled, axis=-1, keepdims=True)  4.52 us
    all_to_all x1, starting transfers between devices, on_device(): lax.all_to_all(back_keys.reshape(dp_count, capacity, patches, kv_width),...  4.35 us
    all_to_all x1, starting transfers between devices, on_device(): lax.all_to_all(route_send.reshape(dp_count, capacity), 'dp', split_axis=0...  4.26 us
    all_to_all x1, starting transfers between devices, on_device(): lax.all_to_all(back_vals.reshape(dp_count, capacity, patches, kv_width),...  4.14 us
    all_to_all x1, waiting for transfers between devices, on_device(): lax.all_to_all(send_vals.reshape(dp_count, capacity, patches, kv_width),...  4.02 us
    all_to_all x1, starting transfers between devices, on_device(): lax.all_to_all(send_vals.reshape(dp_count, capacity, patches, kv_width),...  3.47 us
  transfers between devices with their start and end apart: 5, of which 4 were waited for; matrix products, arithmetic and copies ran while one was open for 18% of the time, Pallas kernels for 0%

commit v1 on v0

v1 whole, which is shorter than its diff:
```python
import functools

import jax
import jax.numpy as jnp
from jax import lax
from jax.experimental import pallas as pl
from jax.experimental.pallas import tpu as pltpu
from jax.sharding import PartitionSpec as P

MESH = pl.DeviceIdType.MESH
AXES = ("mp", "dp", "sec")
F32 = jnp.float32
BF16 = jnp.bfloat16


def dot(a, b, ca, cb):
    return lax.dot_general(a, b, (((ca,), (cb,)), ((), ())), preferred_element_type=F32)


def fold_rows(x):
    return jnp.sum(x.reshape(x.shape[0] // 8, 8, x.shape[1]), axis=0)


def fused(
    dims,
    q_hbm,
    c_hbm,
    k_hbm,
    v_hbm,
    counts,
    route,
    lens,
    q_gain,
    k_gain,
    dq_hbm,
    dk_hbm,
    dv_hbm,
    gq_out,
    gk_out,
    bufs,
    sends,
    recvs,
    grads,
    backs,
    homes,
    parts,
    gathers,
    sems,
    gain_sems,
):
    seq_dev, seq_len, img_dev, patches, heads, group, hd, cap, sizes = dims
    (q_v, c_v, own_k, own_v, xhat_v, rinv_v, qn_v, gr_v, dq_v, dk_v, dv_v) = bufs[:11]
    (acc, route_out, route_in, route_s, slot_own, slot_cell, slot_flag, cell_slot,
     home_slot, home_cell, home_flag) = bufs[11:]
    (in_sem, out_sem, rt_send, rt_recv, rt_local, kv_send, kv_recv, bk_send, bk_recv) = sems
    dp = sizes["dp"]
    me = lax.axis_index("dp")
    scaling = hd ** (-0.5)
    slots = 4 * seq_dev
    first_code = (lax.axis_index("sec") * dp + me) * slots

    def peer(axis, offset):
        return lax.rem(lax.axis_index(axis) + offset, sizes[axis])

    barrier = pltpu.get_barrier_semaphore()
    for axis in AXES:
        for o in range(1, sizes[axis]):
            pl.semaphore_signal(barrier, inc=1, device_id={axis: peer(axis, o)}, device_id_type=MESH)

    in_copies = [
        pltpu.make_async_copy(src, dst, in_sem.at[n])
        for n, (src, dst) in enumerate(((k_hbm, own_k), (v_hbm, own_v), (q_hbm, q_v), (c_hbm, c_v)))
    ]
    for copy in in_copies:
        copy.start()

    lane = lax.broadcasted_iota(jnp.int32, (1, 128), 1)
    codes = [route[i] for i in range(img_dev)]
    packed = jnp.zeros((1, 128), jnp.int32)
    for i in range(img_dev):
        packed = jnp.where(lane == i, codes[i], packed)
    route_out[...] = packed
    target = [lax.rem(lax.div(codes[i], slots), dp) for i in range(img_dev)]

    for i in range(img_dev):
        order = jnp.int32(0)
        for j in range(i):
            order = order + jnp.where(target[j] == target[i], 1, 0)
        mine = target[i] == me
        home_flag[i] = jnp.where(mine, 1, 0)
        home_slot[i] = jnp.where(mine, jnp.clip(codes[i] - first_code, 0, slots - 1), 0)
        home_cell[i] = jnp.where(mine, peer("dp", 1) * cap, target[i] * cap + jnp.minimum(order, cap - 1))

    def send_cells(h, d):
        for c in range(cap):
            image = jnp.int32(0)
            for i in range(img_dev):
                image = jnp.where(home_cell[i] == d * cap + c, jnp.where(target[i] == d, i, image), image)
            sends[h][d, c, 0] = own_k[image, :, h * hd : (h + 1) * hd]
            sends[h][d, c, 1] = own_v[image, :, h * hd : (h + 1) * hd]

    def kv_copy(h, d, slot):
        return pltpu.make_async_remote_copy(
            src_ref=sends[h].at[d],
            dst_ref=recvs[h].at[slot],
            send_sem=kv_send.at[h, d],
            recv_sem=kv_recv.at[h, slot],
            device_id={"dp": d},
            device_id_type=MESH,
        )

    def back_copy(h, d, slot):
        return pltpu.make_async_remote_copy(
            src_ref=backs[h].at[d],
            dst_ref=homes[h].at[slot],
            send_sem=bk_send.at[h, d],
            recv_sem=bk_recv.at[h, slot],
            device_id={"dp": d},
            device_id_type=MESH,
        )

    def route_copy(d, slot):
        return pltpu.make_async_remote_copy(
            src_ref=route_out,
            dst_ref=route_in.at[slot],
            send_sem=rt_send.at[d],
            recv_sem=rt_recv.at[slot],
            device_id={"dp": d},
            device_id_type=MESH,
        )

    def peers(body):
        if dp == 2:
            body(peer("dp", 1))
        else:

            def step(o, carry):
                body(peer("dp", o))
                return carry

            lax.fori_loop(1, dp, step, 0)

    in_copies[0].wait()
    in_copies[1].wait()
    peers(lambda d: send_cells(0, d))
    pl.semaphore_wait(barrier, sum(sizes[a] - 1 for a in AXES))
    peers(lambda d: route_copy(d, me).start())
    peers(lambda d: kv_copy(0, d, me).start())
    for h in range(1, heads):
        peers(lambda d: send_cells(h, d))
        peers(lambda d: kv_copy(h, d, me).start())

    in_copies[2].wait()
    in_copies[3].wait()
    qg = q_gain[...]
    kg = k_gain[...]
    rows = group * seq_len
    row_token = lax.rem(lax.broadcasted_iota(jnp.int32, (rows, 1), 0), seq_len)

    def stack(ref, s, h):
        return jnp.concatenate(
            [
                ref[pl.ds(pl.multiple_of(s * seq_len, seq_len), seq_len), (h * group + g) * hd : (h * group + g + 1) * hd]
                for g in range(group)
            ],
            axis=0,
        )

    def prepare(s, carry):
        for h in range(heads):
            x = stack(q_v, s, h).astype(F32)
            r = lax.rsqrt(jnp.mean(x * x, axis=-1, keepdims=True) + 1e-05)
            xr = x * r
            xhat_v[h, s] = xr
            rinv_v[h, s] = jnp.broadcast_to(r, xr.shape)
            qn_v[h, s] = (xr * qg).astype(BF16)
            grad = stack(c_v, s, h)
            gr_v[h, s] = jnp.where(row_token < lens[s], grad, jnp.zeros_like(grad))
        return carry

    lax.fori_loop(0, seq_dev, prepare, 0)
    acc[...] = jnp.zeros_like(acc)

    for q in range(slots):
        own = jnp.int32(0)
        flag = jnp.int32(0)
        for i in range(img_dev):
            match = codes[i] - first_code == q
            own = jnp.where(match, i, own)
            flag = jnp.where(match, 1, flag)
        slot_own[q] = own
        slot_flag[q] = flag
        slot_cell[q] = peer("dp", 1) * cap

    peers(lambda d: route_copy(d, d).wait_recv())
    peers(lambda d: pltpu.make_async_copy(route_in.at[d], route_s.at[d], rt_local.at[d]).start())
    peers(lambda d: pltpu.make_async_copy(route_in.at[d], route_s.at[d], rt_local.at[d]).wait())

    def scan_source(d):
        run = jnp.int32(0)
        local, place = [], []
        for i in range(img_dev):
            code = route_s[d, 0, i] - first_code
            mine = (code >= 0) & (code < slots)
            local.append(jnp.where(mine, code, -1))
            place.append(jnp.where(mine, jnp.minimum(run, cap - 1), -1))
            run = run + jnp.where(mine, 1, 0)
        for q in range(slots):
            cell = slot_cell[q]
            for i in range(img_dev):
                cell = jnp.where(local[i] == q, d * cap + place[i], cell)
            slot_cell[q] = cell
        for c in range(cap):
            slot = jnp.int32(0)
            for i in range(img_dev):
                slot = jnp.where(place[i] == c, local[i], slot)
            cell_slot[d * cap + c] = slot

    peers(scan_source)

    keys = 4 * patches
    col_image = lax.div(lax.broadcasted_iota(jnp.int32, (1, keys), 1), patches)

    def attend(h, s):
        raw, val = [], []
        for p in range(4):
            n = 4 * s + p
            own, cell = slot_own[n], slot_cell[n]
            mine = slot_flag[n] == 1
            live = p < counts[s]
            cd, cc = lax.div(cell, cap), lax.rem(cell, cap)
            k_one = jnp.where(mine, own_k[own, :, h * hd : (h + 1) * hd], recvs[h][cd, cc, 0])
            v_one = jnp.where(mine, own_v[own, :, h * hd : (h + 1) * hd], recvs[h][cd, cc, 1])
            raw.append(jnp.where(live, k_one, jnp.zeros_like(k_one)))
            val.append(jnp.where(live, v_one, jnp.zeros_like(v_one)))
        kx = jnp.concatenate(raw, axis=0).astype(F32)
        v = jnp.concatenate(val, axis=0)
        kx = kx * lax.rsqrt(jnp.mean(kx * kx, axis=-1, keepdims=True) + 1e-05)
        kn = (kx * kg).astype(BF16)
        qn = qn_v[h, s]
        grad = gr_v[h, s]
        scores = jnp.where(col_image < counts[s], dot(qn, kn, 1, 1) * scaling, -1e30)
        dprob = dot(grad, v, 1, 1)
        expo = jnp.exp(scores - jnp.max(scores, axis=-1, keepdims=True))
        probs = expo * (1.0 / jnp.sum(expo, axis=-1, keepdims=True))
        low = probs.astype(BF16)
        row_dots = jnp.sum(low.astype(F32) * dprob, axis=-1, keepdims=True)
        dscore = (probs * (dprob - row_dots)).astype(BF16)
        dv = dot(low, grad, 0, 0).astype(BF16)
        dk = (dot(dscore, qn, 0, 0) * scaling).astype(BF16)
        dq = dot(dscore, kn, 1, 0) * scaling
        for p in range(4):
            grads[h][4 * s + p, 0] = dk[p * patches : (p + 1) * patches]
            grads[h][4 * s + p, 1] = dv[p * patches : (p + 1) * patches]
        acc[1] += fold_rows(dk.astype(F32) * kx)
        xr = xhat_v[h, s]
        prod = xr * dq
        acc[0] += fold_rows(prod)
        mean = jnp.mean(prod * qg, axis=-1, keepdims=True)
        dx = (rinv_v[h, s] * (dq * qg - xr * mean)).astype(BF16)
        for g in range(group):
            dq_v[
                pl.ds(pl.multiple_of(s * seq_len, seq_len), seq_len),
                (h * group + g) * hd : (h * group + g + 1) * hd,
            ] = dx[g * seq_len : (g + 1) * seq_len]

    def fill_back(h, d):
        for c in range(cap):
            slot = cell_slot[d * cap + c]
            backs[h][d, c] = grads[h][slot]

    out_copies = []
    width = group * hd
    for h in range(heads):
        peers(lambda d: kv_copy(h, d, d).wait_recv())

        def seq_step(s, carry):
            attend(h, s)
            return carry

        lax.fori_loop(0, seq_dev, seq_step, 0)
        peers(lambda d: fill_back(h, d))
        peers(lambda d: back_copy(h, d, me).start())
        copy = pltpu.make_async_copy(
            dq_v.at[:, h * width : (h + 1) * width], dq_hbm.at[:, h * width : (h + 1) * width], out_sem.at[h]
        )
        copy.start()
        out_copies.append(copy)

    def gain_copy(n, o, slot):
        axis = AXES[n]
        return pltpu.make_async_remote_copy(
            src_ref=parts.at[n],
            dst_ref=gathers[n].at[slot],
            send_sem=gain_sems[2 * n].at[o],
            recv_sem=gain_sems[2 * n + 1].at[slot],
            device_id={axis: peer(axis, o)},
            device_id_type=MESH,
        )

    def gain_send(n, value):
        mine = lax.axis_index(AXES[n])
        parts[n] = value
        gathers[n][mine] = value
        for o in range(1, sizes[AXES[n]]):
            gain_copy(n, o, mine).start()

    def gain_recv(n):
        for o in range(1, sizes[AXES[n]]):
            gain_copy(n, o, peer(AXES[n], o)).wait_recv()
        total = gathers[n][0]
        for j in range(1, sizes[AXES[n]]):
            total = total + gathers[n][j]
        return total

    def finish(h):
        peers(lambda d: back_copy(h, d, d).wait_recv())
        for i in range(img_dev):
            cell = home_cell[i]
            cd, cc = lax.div(cell, cap), lax.rem(cell, cap)
            both = jnp.where(home_flag[i] == 1, grads[h][home_slot[i]], homes[h][cd, cc])
            dv_v[i, :, h * hd : (h + 1) * hd] = both[1]
            dy = both[0].astype(F32)
            x = own_k[i, :, h * hd : (h + 1) * hd].astype(F32)
            r = lax.rsqrt(jnp.mean(x * x, axis=-1, keepdims=True) + 1e-05)
            u = kg * dy
            xr = x * r
            dk_v[i, :, h * hd : (h + 1) * hd] = (
                r * (u - xr * jnp.mean(xr * u, axis=-1, keepdims=True))
            ).astype(BF16)

    gain_send(0, jnp.sum(acc[...], axis=1))
    for h in range(heads - 1):
        finish(h)
    gain_send(1, gain_recv(0))
    gain_send(2, gain_recv(1))
    finish(heads - 1)
    for n, (src, dst) in enumerate(((dk_v, dk_hbm), (dv_v, dv_hbm))):
        copy = pltpu.make_async_copy(src, dst, out_sem.at[heads + n])
        copy.start()
        out_copies.append(copy)
    total = gain_recv(2)
    gq_out[...] = total[0:1]
    gk_out[...] = total[1:2]

    for copy in out_copies:
        copy.wait()
    peers(lambda d: route_copy(d, me).wait_send())
    for h in range(heads):
        peers(lambda d: kv_copy(h, d, me).wait_send())
        peers(lambda d: back_copy(h, d, me).wait_send())
    for n in range(len(AXES)):
        for o in range(1, sizes[AXES[n]]):
            gain_copy(n, o, lax.axis_index(AXES[n])).wait_send()


def on_device(
    queries, cotangent, keys_raw, values, image_counts, image_route, text_lengths, q_gain, k_gain
):
    sizes = {axis: lax.axis_size(axis) for axis in AXES}
    dp = sizes["dp"]
    seq_dev = image_counts.shape[0]
    img_dev, patches, kv_width = keys_raw.shape
    hd = q_gain.shape[0]
    heads = kv_width // hd
    tokens = queries.shape[0]
    seq_len = tokens // seq_dev
    group = queries.shape[1] // hd // heads
    cap = (4 * seq_dev + dp - 1) // dp
    slots = 4 * seq_dev
    rows = group * seq_len
    dims = (seq_dev, seq_len, img_dev, patches, heads, group, hd, cap, sizes)
    cells = (dp, cap, 2, patches, hd)
    vmem, smem, dma = pltpu.VMEM, pltpu.SMEM, pltpu.SemaphoreType.DMA
    unit = (heads, seq_dev, rows, hd)
    scratch = [
        [
            vmem(queries.shape, BF16),
            vmem(queries.shape, BF16),
            vmem(keys_raw.shape, BF16),
            vmem(keys_raw.shape, BF16),
            vmem(unit, F32),
            vmem(unit, F32),
            vmem(unit, BF16),
            vmem(unit, BF16),
            vmem(queries.shape, BF16),
            vmem(keys_raw.shape, BF16),
            vmem(keys_raw.shape, BF16),
            vmem((2, 8, hd), F32),
            vmem((1, 128), jnp.int32),
            vmem((dp, 1, 128), jnp.int32),
            smem((dp, 1, 128), jnp.int32),
            smem((slots,), jnp.int32),
            smem((slots,), jnp.int32),
            smem((slots,), jnp.int32),
            smem((dp * cap,), jnp.int32),
            smem((img_dev,), jnp.int32),
            smem((img_dev,), jnp.int32),
            smem((img_dev,), jnp.int32),
        ],
        [vmem(cells, BF16) for _ in range(heads)],
        [vmem(cells, BF16) for _ in range(heads)],
        [vmem((slots, 2, patches, hd), BF16) for _ in range(heads)],
        [vmem(cells, BF16) for _ in range(heads)],
        [vmem(cells, BF16) for _ in range(heads)],
        vmem((len(AXES), 2, hd), F32),
        [vmem((sizes[a], 2, hd), F32) for a in AXES],
        [
            dma((4,)),
            dma((heads + 2,)),
            dma((dp,)),
            dma((dp,)),
            dma((dp,)),
            dma((heads, dp)),
            dma((heads, dp)),
            dma((heads, dp)),
            dma((heads, dp)),
        ],
        [dma((sizes[a],)) for a in AXES for _ in range(2)],
    ]
    hbm = pl.BlockSpec(memory_space=pl.ANY)
    in_smem = pl.BlockSpec(memory_space=pltpu.SMEM)
    in_vmem = pl.BlockSpec(memory_space=pltpu.VMEM)
    query_grad, key_grad, value_grad, gq, gk = pl.pallas_call(
        functools.partial(fused, dims),
        out_shape=(
            jax.ShapeDtypeStruct(queries.shape, BF16),
            jax.ShapeDtypeStruct(keys_raw.shape, BF16),
            jax.ShapeDtypeStruct(values.shape, BF16),
            jax.ShapeDtypeStruct((1, hd), F32),
            jax.ShapeDtypeStruct((1, hd), F32),
        ),
        in_specs=[hbm] * 4 + [in_smem] * 3 + [in_vmem] * 2,
        out_specs=(hbm, hbm, hbm, in_vmem, in_vmem),
        scratch_shapes=scratch,
        compiler_params=pltpu.CompilerParams(collective_id=0, has_side_effects=True),
        name="relay_attention",
    )(
        queries,
        cotangent,
        keys_raw,
        values,
        image_counts,
        image_route,
        text_lengths,
        q_gain.reshape(1, hd),
        k_gain.reshape(1, hd),
    )
    return (query_grad, key_grad, value_grad, gq.reshape(hd), gk.reshape(hd))


def solution(mesh):
    placed = (
        P(("sec", "dp"), "mp"),
        P(("sec", "dp"), "mp"),
        P(("sec", "dp"), None, "mp"),
        P(("sec", "dp"), None, "mp"),
        P(("sec", "dp")),
        P(("sec", "dp")),
        P(("sec", "dp")),
        P(),
        P(),
    )
    return jax.shard_map(
        on_device,
        mesh=mesh,
        in_specs=placed,
        out_specs=(
            P(("sec", "dp"), "mp"),
            P(("sec", "dp"), None, "mp"),
            P(("sec", "dp"), None, "mp"),
            P(),
            P(),
        ),
        check_vma=False,
    )
```

time: 111 us -> 35.6 us (0.32)
  blocking collectives: 40.2 us -> 0 us
  Pallas kernels: 0 us -> 30 us
  starting transfers between devices: 19.7 us -> 0 us
  local copies, waits for them, and re-layouts: 19.2 us -> 4.74 us
  matrix products: 11.5 us -> 0 us
  waiting for transfers between devices: 11.4 us -> 0 us
  other arithmetic: 7.4 us -> 0 us
    psum x1 -> x0, blocking collectives: 40.2 us -> none  [on_device(): q_gain_grad, k_gain_grad = lax.psum((q_part, k_part), ('sec', 'dp', 'mp'))]
    pallas_call x0 -> x1, Pallas kernels: none -> 30 us  [on_device(): pl.pallas_call(functools.partial(fused, dims), out_shape=(jax.ShapeDtypeS...]
    all_to_all x5 -> x0, starting transfers between devices: 19.7 us -> none  [the longest x1 4.35 us: on_device(): lax.all_to_all(back_keys.reshape(dp_count, capacity, patches, kv_width),...]
    dot_general x14 -> x0, matrix products: 11.5 us -> none  [the longest x1 1.84 us: attend(): jnp.einsum('skglj,slkgd->sjkd', probs_low, grad, preferred_element_type=j...]
    all_to_all x5 -> x0, waiting for transfers between devices: 11.4 us -> none  [the longest x1 4.81 us: on_device(): lax.all_to_all(send_keys.reshape(dp_count, capacity, patches, kv_width),...]
    reshape x9 -> x0, local copies, waits for them, and re-layouts: 7.32 us -> none  [the longest x1 1.99 us: on_device(): dk_slots.reshape(4 * seq_dev, patches, kv_width)]
    mul x8 -> x0, local copies, waits for them, and re-layouts: 6.3 us -> none  [the longest x4 4.52 us: norm_backward(): wide * inv_rms ** 3 * jnp.mean(wide * scaled, axis=-1, keepdims=True)]
    unnamed x33 -> x13, local copies, waits for them, and re-layouts: 2.16 us -> 4.74 us
  transfers between devices with their start and end apart: 5 -> 0, of which waited for: 4 -> 0; matrix products, arithmetic and copies ran while one was open for 18% -> 0% of each run, Pallas kernels for 0% -> 0%
where the time goes in v1:
time: 35.6 us; the launch traced here: 35.4 us
  Pallas kernels  30 us (84%)
  local copies, waits for them, and re-layouts  4.74 us (13%)
  between operations  0.66 us (2%)
    pallas_call x1, Pallas kernels, on_device(): pl.pallas_call(functools.partial(fused, dims), out_shape=(jax.ShapeDtypeS...  30 us
    unnamed x13, local copies, waits for them, and re-layouts  4.74 us

profile of v1, /device:TPU:0, one launch (start us, length us, event | category | flops | bytes accessed | tf_op | source)
XLA Modules:
  0.0 35.4 jit_solution(2816901727510026567)
XLA Ops:
  0.6 30.0 %relay_attention.1 = (bf16[128,2048]{1,0:T(8,128)(2,1)}, bf16[10,48,256]{2,1,0:T(8,128)(2,1)}, bf16[10,48,256]{2,1,0:T(8,128)(2,1)}, f32[1,128]{1,0:T(1,128)}, f32[1,128]{1,0:T(1,128)}) custom-call(bf16[128,2048]{1,0:T(8,128)(2,1)} %q_hbm.1, bf16[128,2048]{1,0:T(8,128)(2,1)} %c_hbm.1, bf16[10,48,256]{2,1,0:T(8,128)(2,1)} %k_hbm.1, ...), custom_call_target="tpu_custom_call" | custom-call | tf_op jit(solution)/shard_map/relay_attention/pallas_call | solution.py:424
  30.6 0.0 copy-start.1
  30.6 1.9 %copy.19 = bf16[128,2048]{1,0:T(8,128)(2,1)} copy(bf16[128,2048]{1,0:T(8,128)(2,1)} %get-tuple-element.20) | data formatting | bytes 1048576
  32.6 0.0 copy-done.1
  32.6 0.0 copy-start
  32.6 0.7 %copy.20 = bf16[10,48,256]{2,1,0:T(8,128)(2,1)} copy(bf16[10,48,256]{2,1,0:T(8,128)(2,1)S(1)} %copy-done.1) | data formatting | bytes 491520
  33.3 0.3 copy-done
  33.6 0.0 copy-start.3
  33.6 0.7 %copy.21 = bf16[10,48,256]{2,1,0:T(8,128)(2,1)} copy(bf16[10,48,256]{2,1,0:T(8,128)(2,1)S(1)} %copy-done) | data formatting | bytes 491520
  34.3 0.0 copy-done.3
  34.3 0.0 copy-start.2
  34.3 0.5 %copy.22 = f32[128]{0:T(128)} copy(f32[128]{0:T(128)S(1)} %bitcast.7) | data formatting | bytes 1024
  34.8 0.1 copy-done.2
  34.9 0.5 %copy.23 = f32[128]{0:T(128)} copy(f32[128]{0:T(128)S(1)} %bitcast.6) | data formatting | bytes 1024
Async XLA Ops:
  30.6 1.9 %copy-start.1 = (bf16[10,48,256]{2,1,0:T(8,128)(2,1)S(1)}, bf16[10,48,256]{2,1,0:T(8,128)(2,1)}, u32[]{:S(2)}) copy-start(bf16[10,48,256]{2,1,0:T(8,128)(2,1)} %get-tuple-element.21) | copy-start | bytes 737284
  32.6 1.0 %copy-start = (bf16[10,48,256]{2,1,0:T(8,128)(2,1)S(1)}, bf16[10,48,256]{2,1,0:T(8,128)(2,1)}, u32[]{:S(2)}) copy-start(bf16[10,48,256]{2,1,0:T(8,128)(2,1)} %get-tuple-element.22) | copy-start | bytes 737284
  33.6 0.7 %copy-start.3 = (f32[1,128]{1,0:T(1,128)S(1)}, f32[1,128]{1,0:T(1,128)}, u32[]{:S(2)}) copy-start(f32[1,128]{1,0:T(1,128)} %get-tuple-element.13) | copy-start | bytes 1540
  34.3 0.6 %copy-start.2 = (f32[1,128]{1,0:T(1,128)S(1)}, f32[1,128]{1,0:T(1,128)}, u32[]{:S(2)}) copy-start(f32[1,128]{1,0:T(1,128)} %get-tuple-element.14) | copy-start | bytes 1540

commit v2 on v1

--- a/solution.py
+++ b/solution.py
@@ -8,7 +8,7 @@
 from jax.sharding import PartitionSpec as P
 
 MESH = pl.DeviceIdType.MESH
-AXES = ("mp", "dp", "sec")
+AXES = ("dp", "mp", "sec")
 F32 = jnp.float32
 BF16 = jnp.bfloat16
 
@@ -27,14 +27,14 @@
     c_hbm,
     k_hbm,
     v_hbm,
-    counts,
-    route,
-    lens,
-    q_gain,
-    k_gain,
-    dq_hbm,
-    dk_hbm,
-    dv_hbm,
+    counts_hbm,
+    route_hbm,
+    lens_hbm,
+    q_gain_hbm,
+    k_gain_hbm,
+    dq_v,
+    dk_v,
+    dv_v,
     gq_out,
     gk_out,
     bufs,
@@ -49,10 +49,11 @@
     gain_sems,
 ):
     seq_dev, seq_len, img_dev, patches, heads, group, hd, cap, sizes = dims
-    (q_v, c_v, own_k, own_v, xhat_v, rinv_v, qn_v, gr_v, dq_v, dk_v, dv_v) = bufs[:11]
+    (q_v, c_v, own_k, own_v, xhat_v, rinv_v, qn_v, gr_v, counts, route, lens) = bufs[:11]
+    q_gain, k_gain = bufs[22:]
     (acc, route_out, route_in, route_s, slot_own, slot_cell, slot_flag, cell_slot,
-     home_slot, home_cell, home_flag) = bufs[11:]
-    (in_sem, out_sem, rt_send, rt_recv, rt_local, kv_send, kv_recv, bk_send, bk_recv) = sems
+     home_slot, home_cell, home_flag) = bufs[11:22]
+    (in_sem, rt_send, rt_recv, rt_local, kv_send, kv_recv, bk_send, bk_recv) = sems
     dp = sizes["dp"]
     me = lax.axis_index("dp")
     scaling = hd ** (-0.5)
@@ -69,12 +70,25 @@
 
     in_copies = [
         pltpu.make_async_copy(src, dst, in_sem.at[n])
-        for n, (src, dst) in enumerate(((k_hbm, own_k), (v_hbm, own_v), (q_hbm, q_v), (c_hbm, c_v)))
+        for n, (src, dst) in enumerate(
+            (
+                (route_hbm, route),
+                (k_hbm, own_k),
+                (v_hbm, own_v),
+                (q_hbm, q_v),
+                (c_hbm, c_v),
+                (counts_hbm, counts),
+                (lens_hbm, lens),
+                (q_gain_hbm, q_gain),
+                (k_gain_hbm, k_gain),
+            )
+        )
     ]
     for copy in in_copies:
         copy.start()
 
     lane = lax.broadcasted_iota(jnp.int32, (1, 128), 1)
+    in_copies[0].wait()
     codes = [route[i] for i in range(img_dev)]
     packed = jnp.zeros((1, 128), jnp.int32)
     for i in range(img_dev):
@@ -140,8 +154,8 @@
 
             lax.fori_loop(1, dp, step, 0)
 
-    in_copies[0].wait()
     in_copies[1].wait()
+    in_copies[2].wait()
     peers(lambda d: send_cells(0, d))
     pl.semaphore_wait(barrier, sum(sizes[a] - 1 for a in AXES))
     peers(lambda d: route_copy(d, me).start())
@@ -150,8 +164,8 @@
         peers(lambda d: send_cells(h, d))
         peers(lambda d: kv_copy(h, d, me).start())
 
-    in_copies[2].wait()
-    in_copies[3].wait()
+    for copy in in_copies[3:]:
+        copy.wait()
     qg = q_gain[...]
     kg = k_gain[...]
     rows = group * seq_len
@@ -269,24 +283,6 @@
             slot = cell_slot[d * cap + c]
             backs[h][d, c] = grads[h][slot]
 
-    out_copies = []
-    width = group * hd
-    for h in range(heads):
-        peers(lambda d: kv_copy(h, d, d).wait_recv())
-
-        def seq_step(s, carry):
-            attend(h, s)
-            return carry
-
-        lax.fori_loop(0, seq_dev, seq_step, 0)
-        peers(lambda d: fill_back(h, d))
-        peers(lambda d: back_copy(h, d, me).start())
-        copy = pltpu.make_async_copy(
-            dq_v.at[:, h * width : (h + 1) * width], dq_hbm.at[:, h * width : (h + 1) * width], out_sem.at[h]
-        )
-        copy.start()
-        out_copies.append(copy)
-
     def gain_copy(n, o, slot):
         axis = AXES[n]
         return pltpu.make_async_remote_copy(
@@ -312,6 +308,19 @@
         for j in range(1, sizes[AXES[n]]):
             total = total + gathers[n][j]
         return total
+
+    for h in range(heads):
+        peers(lambda d: kv_copy(h, d, d).wait_recv())
+
+        def seq_step(s, carry):
+            attend(h, s)
+            return carry
+
+        lax.fori_loop(0, seq_dev, seq_step, 0)
+        if h == heads - 1:
+            gain_send(0, jnp.sum(acc[...], axis=1))
+        peers(lambda d: fill_back(h, d))
+        peers(lambda d: back_copy(h, d, me).start())
 
     def finish(h):
         peers(lambda d: back_copy(h, d, d).wait_recv())
@@ -329,22 +338,15 @@
                 r * (u - xr * jnp.mean(xr * u, axis=-1, keepdims=True))
             ).astype(BF16)
 
-    gain_send(0, jnp.sum(acc[...], axis=1))
+    gain_send(1, gain_recv(0))
     for h in range(heads - 1):
         finish(h)
-    gain_send(1, gain_recv(0))
     gain_send(2, gain_recv(1))
     finish(heads - 1)
-    for n, (src, dst) in enumerate(((dk_v, dk_hbm), (dv_v, dv_hbm))):
-        copy = pltpu.make_async_copy(src, dst, out_sem.at[heads + n])
-        copy.start()
-        out_copies.append(copy)
     total = gain_recv(2)
     gq_out[...] = total[0:1]
     gk_out[...] = total[1:2]
 
-    for copy in out_copies:
-        copy.wait()
     peers(lambda d: route_copy(d, me).wait_send())
     for h in range(heads):
         peers(lambda d: kv_copy(h, d, me).wait_send())
@@ -352,6 +354,14 @@
     for n in range(len(AXES)):
         for o in range(1, sizes[AXES[n]]):
             gain_copy(n, o, lax.axis_index(AXES[n])).wait_send()
+
+
+def put_out(*refs):
+    copies = [pltpu.make_async_copy(refs[n], refs[5 + n], refs[10].at[n]) for n in range(5)]
+    for copy in copies:
+        copy.start()
+    for copy in copies:
+        copy.wait()
 
 
 def on_device(
@@ -383,9 +393,9 @@
             vmem(unit, F32),
             vmem(unit, BF16),
             vmem(unit, BF16),
-            vmem(queries.shape, BF16),
-            vmem(keys_raw.shape, BF16),
-            vmem(keys_raw.shape, BF16),
+            smem((seq_dev,), jnp.int32),
+            smem((img_dev,), jnp.int32),
+            smem((seq_dev,), jnp.int32),
             vmem((2, 8, hd), F32),
             vmem((1, 128), jnp.int32),
             vmem((dp, 1, 128), jnp.int32),
@@ -397,6 +407,8 @@
             smem((img_dev,), jnp.int32),
             smem((img_dev,), jnp.int32),
             smem((img_dev,), jnp.int32),
+            vmem((1, hd), F32),
+            vmem((1, hd), F32),
         ],
         [vmem(cells, BF16) for _ in range(heads)],
         [vmem(cells, BF16) for _ in range(heads)],
@@ -406,8 +418,7 @@
         vmem((len(AXES), 2, hd), F32),
         [vmem((sizes[a], 2, hd), F32) for a in AXES],
         [
-            dma((4,)),
-            dma((heads + 2,)),
+            dma((9,)),
             dma((dp,)),
             dma((dp,)),
             dma((dp,)),
@@ -419,23 +430,15 @@
         [dma((sizes[a],)) for a in AXES for _ in range(2)],
     ]
     hbm = pl.BlockSpec(memory_space=pl.ANY)
-    in_smem = pl.BlockSpec(memory_space=pltpu.SMEM)
     in_vmem = pl.BlockSpec(memory_space=pltpu.VMEM)
-    query_grad, key_grad, value_grad, gq, gk = pl.pallas_call(
-        functools.partial(fused, dims),
-        out_shape=(
-            jax.ShapeDtypeStruct(queries.shape, BF16),
-            jax.ShapeDtypeStruct(keys_raw.shape, BF16),
-            jax.ShapeDtypeStruct(values.shape, BF16),
-            jax.ShapeDtypeStruct((1, hd), F32),
-            jax.ShapeDtypeStruct((1, hd), F32),
-        ),
-        in_specs=[hbm] * 4 + [in_smem] * 3 + [in_vmem] * 2,
-        out_specs=(hbm, hbm, hbm, in_vmem, in_vmem),
-        scratch_shapes=scratch,
-        compiler_params=pltpu.CompilerParams(collective_id=0, has_side_effects=True),
-        name="relay_attention",
-    )(
+    shapes = (
+        (queries.shape, BF16),
+        (keys_raw.shape, BF16),
+        (values.shape, BF16),
+        ((1, hd), F32),
+        ((1, hd), F32),
+    )
+    operands = (
         queries,
         cotangent,
         keys_raw,
@@ -446,6 +449,24 @@
         q_gain.reshape(1, hd),
         k_gain.reshape(1, hd),
     )
+    results = pl.pallas_call(
+        functools.partial(fused, dims),
+        out_shape=tuple(pltpu.VMEM(shape, dtype) for shape, dtype in shapes),
+        in_specs=[pl.BlockSpec(memory_space=pltpu.HBM)] * 9,
+        out_specs=(in_vmem,) * 5,
+        scratch_shapes=scratch,
+        compiler_params=pltpu.CompilerParams(collective_id=0, has_side_effects=True, vmem_limit_bytes=40 * 2**20),
+        name="relay_attention",
+    )(*[pltpu.with_memory_space_constraint(x, pltpu.HBM) for x in operands])
+    query_grad, key_grad, value_grad, gq, gk = pl.pallas_call(
+        put_out,
+        out_shape=tuple(jax.ShapeDtypeStruct(shape, dtype) for shape, dtype in shapes),
+        in_specs=[hbm] * 5,
+        out_specs=(hbm,) * 5,
+        scratch_shapes=[dma((5,))],
+        compiler_params=pltpu.CompilerParams(vmem_limit_bytes=2**20),
+        name="put_out",
+    )(*results)
     return (query_grad, key_grad, value_grad, gq.reshape(hd), gk.reshape(hd))
 
 

time: 35.6 us -> 30.5 us (0.86)
  local copies, waits for them, and re-layouts: 4.74 us -> 0 us
    unnamed x13 -> x0, local copies, waits for them, and re-layouts: 4.74 us -> none
    pallas_call x1 -> x2, Pallas kernels: 30 us -> 29.7 us  [the longest x1 28.7 us: on_device(): pl.pallas_call(functools.partial(fused, dims), out_shape=tuple((pltpu.VME...]
where the time goes in v2:
time: 30.5 us; the launch traced here: 30.3 us
  Pallas kernels  29.7 us (97%)
  between operations  0.64 us (2%)
    pallas_call x1, Pallas kernels, on_device(): pl.pallas_call(functools.partial(fused, dims), out_shape=tuple((pltpu.VME...  28.7 us
    pallas_call x1, Pallas kernels, on_device(): pl.pallas_call(put_out, out_shape=tuple((jax.ShapeDtypeStruct(shape, dtyp...  1 us

profile of v2, /device:TPU:0, one launch (start us, length us, event | category | flops | bytes accessed | tf_op | source)
XLA Modules:
  0.0 30.3 jit_solution(9343789929436126233)
XLA Ops:
  0.6 28.7 %relay_attention.1 = (bf16[128,2048]{1,0:T(8,128)(2,1)S(1)}, bf16[10,48,256]{2,1,0:T(8,128)(2,1)S(1)}, bf16[10,48,256]{2,1,0:T(8,128)(2,1)S(1)}, f32[1,128]{1,0:T(1,128)S(1)}, f32[1,128]{1,0:T(1,128)S(1)}) custom-call(bf16[128,2048]{1,0:T(8,128)(2,1)} %q_hbm.1, bf16[128,2048]{1,0:T(8,128)(2,1)} %c_hbm.1, bf16[10,48,256]{2,1,0:T(8,128)(2,1)} %k_hbm.1, ...), custom_call_target="tpu_custom_call" | custom-call | tf_op jit(solution)/shard_map/relay_attention/pallas_call | solution.py:452
  29.3 1.0 %put_out.1 = (bf16[128,2048]{1,0:T(8,128)(2,1)}, bf16[10,48,256]{2,1,0:T(8,128)(2,1)}, bf16[10,48,256]{2,1,0:T(8,128)(2,1)}, f32[1,128]{1,0:T(1,128)}, f32[1,128]{1,0:T(1,128)}) custom-call(bf16[128,2048]{1,0:T(8,128)(2,1)S(1)} %get-tuple-element.15.refs_0_, bf16[10,48,256]{2,1,0:T(8,128)(2,1)S(1)} %get-tuple-element.16.refs_1_, ...), custom_call_target="tpu_custom_call" | custom-call | tf_op jit(solution)/shard_map/put_out/pallas_call | solution.py:461

commit v3 on v2

--- a/solution.py
+++ b/solution.py
@@ -9,6 +9,7 @@
 
 MESH = pl.DeviceIdType.MESH
 AXES = ("dp", "mp", "sec")
+PLANE, LINE = 0, 1
 F32 = jnp.float32
 BF16 = jnp.bfloat16
 
@@ -47,6 +48,8 @@
     gathers,
     sems,
     gain_sems,
+    from_left,
+    from_right,
 ):
     seq_dev, seq_len, img_dev, patches, heads, group, hd, cap, sizes = dims
     (q_v, c_v, own_k, own_v, xhat_v, rinv_v, qn_v, gr_v, counts, route, lens) = bufs[:11]
@@ -64,9 +67,34 @@
         return lax.rem(lax.axis_index(axis) + offset, sizes[axis])
 
     barrier = pltpu.get_barrier_semaphore()
-    for axis in AXES:
-        for o in range(1, sizes[axis]):
-            pl.semaphore_signal(barrier, inc=1, device_id={axis: peer(axis, o)}, device_id_type=MESH)
+    line_me, line_n = lax.axis_index("mp"), sizes["mp"]
+    plane_n = dp * sizes["sec"]
+    has_left, has_right = line_me > 0, line_me < line_n - 1
+
+    def plane_id(o):
+        return {"dp": peer("dp", lax.rem(o, dp)), "sec": peer("sec", lax.div(o, dp))}
+
+    def plane_slot(where):
+        return where["sec"] * dp + where["dp"]
+
+    def plane_peers(body):
+        if plane_n <= 8:
+            for o in range(1, plane_n):
+                body(plane_id(jnp.int32(o)))
+        else:
+
+            def step(o, carry):
+                body(plane_id(o))
+                return carry
+
+            lax.fori_loop(1, plane_n, step, 0)
+
+    def tell(sem, where):
+        pl.semaphore_signal(sem, inc=1, device_id=where, device_id_type=MESH)
+
+    plane_peers(lambda where: tell(barrier, where))
+    pl.when(has_left)(lambda: tell(barrier, {"mp": line_me - 1}))
+    pl.when(has_right)(lambda: tell(barrier, {"mp": line_me + 1}))
 
     in_copies = [
         pltpu.make_async_copy(src, dst, in_sem.at[n])
@@ -157,7 +185,9 @@
     in_copies[1].wait()
     in_copies[2].wait()
     peers(lambda d: send_cells(0, d))
-    pl.semaphore_wait(barrier, sum(sizes[a] - 1 for a in AXES))
+    pl.semaphore_wait(
+        barrier, plane_n - 1 + jnp.where(has_left, 1, 0) + jnp.where(has_right, 1, 0)
+    )
     peers(lambda d: route_copy(d, me).start())
     peers(lambda d: kv_copy(0, d, me).start())
     for h in range(1, heads):
@@ -194,6 +224,10 @@
 
     lax.fori_loop(0, seq_dev, prepare, 0)
     acc[...] = jnp.zeros_like(acc)
+    pl.when(has_left)(lambda: pl.semaphore_wait(from_left, 1))
+    pl.when(has_right)(lambda: tell(from_left, {"mp": line_me + 1}))
+    pl.when(has_right)(lambda: pl.semaphore_wait(from_right, 1))
+    pl.when(has_left)(lambda: tell(from_right, {"mp": line_me - 1}))
 
     for q in range(slots):
         own = jnp.int32(0)
@@ -283,31 +317,47 @@
             slot = cell_slot[d * cap + c]
             backs[h][d, c] = grads[h][slot]
 
-    def gain_copy(n, o, slot):
-        axis = AXES[n]
+    def plane_copy(where, slot):
         return pltpu.make_async_remote_copy(
-            src_ref=parts.at[n],
-            dst_ref=gathers[n].at[slot],
-            send_sem=gain_sems[2 * n].at[o],
-            recv_sem=gain_sems[2 * n + 1].at[slot],
-            device_id={axis: peer(axis, o)},
+            src_ref=parts.at[PLANE],
+            dst_ref=gathers[PLANE].at[slot],
+            send_sem=gain_sems[0].at[plane_slot(where)],
+            recv_sem=gain_sems[1].at[slot],
+            device_id=where,
             device_id_type=MESH,
         )
 
-    def gain_send(n, value):
-        mine = lax.axis_index(AXES[n])
-        parts[n] = value
-        gathers[n][mine] = value
-        for o in range(1, sizes[AXES[n]]):
-            gain_copy(n, o, mine).start()
-
-    def gain_recv(n):
-        for o in range(1, sizes[AXES[n]]):
-            gain_copy(n, o, peer(AXES[n], o)).wait_recv()
-        total = gathers[n][0]
-        for j in range(1, sizes[AXES[n]]):
-            total = total + gathers[n][j]
-        return total
+    def line_copy(o, slot):
+        return pltpu.make_async_remote_copy(
+            src_ref=parts.at[LINE],
+            dst_ref=gathers[LINE].at[slot],
+            send_sem=gain_sems[2].at[o],
+            recv_sem=gain_sems[3].at[slot],
+            device_id={"mp": peer("mp", o)},
+            device_id_type=MESH,
+        )
+
+    plane_me = plane_slot({"dp": me, "sec": lax.axis_index("sec")})
+
+    def plane_send(value):
+        parts[PLANE] = value
+        gathers[PLANE][plane_me] = value
+        plane_peers(lambda where: plane_copy(where, plane_me).start())
+
+    def plane_recv():
+        plane_peers(lambda where: plane_copy(where, plane_slot(where)).wait_recv())
+        return jnp.sum(gathers[PLANE][...], axis=0)
+
+    def line_send(value):
+        parts[LINE] = value
+        gathers[LINE][line_me] = value
+        for o in range(1, line_n):
+            line_copy(o, line_me).start()
+
+    def line_recv():
+        for o in range(1, line_n):
+            line_copy(o, peer("mp", o)).wait_recv()
+        return jnp.sum(gathers[LINE][...], axis=0)
 
     for h in range(heads):
         peers(lambda d: kv_copy(h, d, d).wait_recv())
@@ -318,7 +368,7 @@
 
         lax.fori_loop(0, seq_dev, seq_step, 0)
         if h == heads - 1:
-            gain_send(0, jnp.sum(acc[...], axis=1))
+            plane_send(jnp.sum(acc[...], axis=1))
         peers(lambda d: fill_back(h, d))
         peers(lambda d: back_copy(h, d, me).start())
 
@@ -338,12 +388,11 @@
                 r * (u - xr * jnp.mean(xr * u, axis=-1, keepdims=True))
             ).astype(BF16)
 
-    gain_send(1, gain_recv(0))
     for h in range(heads - 1):
         finish(h)
-    gain_send(2, gain_recv(1))
+    line_send(plane_recv())
     finish(heads - 1)
-    total = gain_recv(2)
+    total = line_recv()
     gq_out[...] = total[0:1]
     gk_out[...] = total[1:2]
 
@@ -351,9 +400,9 @@
     for h in range(heads):
         peers(lambda d: kv_copy(h, d, me).wait_send())
         peers(lambda d: back_copy(h, d, me).wait_send())
-    for n in range(len(AXES)):
-        for o in range(1, sizes[AXES[n]]):
-            gain_copy(n, o, lax.axis_index(AXES[n])).wait_send()
+    plane_peers(lambda where: plane_copy(where, plane_me).wait_send())
+    for o in range(1, line_n):
+        line_copy(o, line_me).wait_send()
 
 
 def put_out(*refs):
@@ -415,8 +464,8 @@
         [vmem((slots, 2, patches, hd), BF16) for _ in range(heads)],
         [vmem(cells, BF16) for _ in range(heads)],
         [vmem(cells, BF16) for _ in range(heads)],
-        vmem((len(AXES), 2, hd), F32),
-        [vmem((sizes[a], 2, hd), F32) for a in AXES],
+        vmem((2, 2, hd), F32),
+        [vmem((dp * sizes["sec"], 2, hd), F32), vmem((sizes["mp"], 2, hd), F32)],
         [
             dma((9,)),
             dma((dp,)),
@@ -427,7 +476,9 @@
             dma((heads, dp)),
             dma((heads, dp)),
         ],
-        [dma((sizes[a],)) for a in AXES for _ in range(2)],
+        [dma((n,)) for n in (dp * sizes["sec"], sizes["mp"]) for _ in range(2)],
+        pltpu.SemaphoreType.REGULAR,
+        pltpu.SemaphoreType.REGULAR,
     ]
     hbm = pl.BlockSpec(memory_space=pl.ANY)
     in_vmem = pl.BlockSpec(memory_space=pltpu.VMEM)

time: 30.5 us -> 28.5 us (0.934)
  Pallas kernels: 29.7 us -> 27.7 us
    pallas_call x1, Pallas kernels: 28.7 us -> 26.7 us  [on_device(): pl.pallas_call(functools.partial(fused, dims), out_shape=tuple((pltpu.VME...]
where the time goes in v3:
time: 28.5 us; the launch traced here: 28.3 us
  Pallas kernels  27.7 us (97%)
  between operations  0.64 us (2%)
    pallas_call x1, Pallas kernels, on_device(): pl.pallas_call(functools.partial(fused, dims), out_shape=tuple((pltpu.VME...  26.7 us
    pallas_call x1, Pallas kernels, on_device(): pl.pallas_call(put_out, out_shape=tuple((jax.ShapeDtypeStruct(shape, dtyp...  1 us

profile of v3, /device:TPU:0, one launch (start us, length us, event | category | flops | bytes accessed | tf_op | source)
XLA Modules:
  0.0 28.3 jit_solution(13993090024023751948)
XLA Ops:
  0.6 26.7 %relay_attention.1 = (bf16[128,2048]{1,0:T(8,128)(2,1)S(1)}, bf16[10,48,256]{2,1,0:T(8,128)(2,1)S(1)}, bf16[10,48,256]{2,1,0:T(8,128)(2,1)S(1)}, f32[1,128]{1,0:T(1,128)S(1)}, f32[1,128]{1,0:T(1,128)S(1)}) custom-call(bf16[128,2048]{1,0:T(8,128)(2,1)} %q_hbm.1, bf16[128,2048]{1,0:T(8,128)(2,1)} %c_hbm.1, bf16[10,48,256]{2,1,0:T(8,128)(2,1)} %k_hbm.1, ...), custom_call_target="tpu_custom_call" | custom-call | tf_op jit(solution)/shard_map/relay_attention/pallas_call | solution.py:503
  27.3 1.0 %put_out.1 = (bf16[128,2048]{1,0:T(8,128)(2,1)}, bf16[10,48,256]{2,1,0:T(8,128)(2,1)}, bf16[10,48,256]{2,1,0:T(8,128)(2,1)}, f32[1,128]{1,0:T(1,128)}, f32[1,128]{1,0:T(1,128)}) custom-call(bf16[128,2048]{1,0:T(8,128)(2,1)S(1)} %get-tuple-element.15.refs_0_, bf16[10,48,256]{2,1,0:T(8,128)(2,1)S(1)} %get-tuple-element.16.refs_1_, ...), custom_call_target="tpu_custom_call" | custom-call | tf_op jit(solution)/shard_map/put_out/pallas_call | solution.py:512
